TPU v7x, 32 devices: a whole 2x2x4 slice. The times are simulated.
32 devices in a mesh: grp: 4 (over y, x), own: 8 (over z, core).
Axes of the slice: x: 2, y: 2, z: 4, core: 2. Of those that a mesh axis runs over, the one named last changes fastest.
Arguments:
- embeddings: float32 [24576, 768], P(('grp', 'own')), may hold values from -64 to 64
- cluster_ids: int32 [24576], P(('grp', 'own')), may hold values from 0 to 127, as said below
- owner_map: int32 [128], replicated, may hold values from 0 to 7, as said below
- source_order: int32 [24576], P(('grp', 'own')), may hold values from 0 to 767, as said below
Outputs:
- dup_score: float32 [24576], P(('grp', 'own'))
- centroids: float32 [128, 768], P('own')
Inputs may be any that keep to these rules, and one draw needn't show every extreme that they name: `owner_map`: every owner index is given to exactly 16 clusters. `cluster_ids`: within the 768 rows of one device, at most 192 rows have clusters of one owner index; in every draw some owner index receives exactly 192 rows from every device, and every device sends exactly 192 rows to some owner index. Cluster sizes are uneven and some clusters may be empty. `source_order`: each aligned block of 768 entries is a permutation of 0 to 767.
All inputs are finite; a program needn't handle non-finite values.
Results may differ from a plain program's by a relative error of at most 0.0003.
Values sent between devices are 32-bit elements; how exact they have to be, the bound alone decides.
No kernel may reach another device: no remote copies, remote signals or barrier semaphores. Data moves between devices by JAX's collectives and lax.ppermute only.
A program may use at most 128 MiB of HBM per device.

v0:
```python
import jax
import jax.numpy as jnp
from jax import lax
from jax.sharding import PartitionSpec as P

CL_OWN = 16
sharpness = 6.0


def passed_along(value, axis, steps):
    count = lax.axis_size(axis)
    pairs = [(source, (source + steps) % count) for source in range(count)]
    return lax.ppermute(value, axis, pairs)


def unit_rows(embeddings):
    squares = jnp.sum(embeddings * embeddings, axis=1, keepdims=True)
    return embeddings * lax.rsqrt(squares + 1e-06)


def owner_positions(owner_map):
    cluster_index = jnp.arange(owner_map.shape[0], dtype=jnp.int32)
    same_owner = owner_map[:, None] == owner_map[None, :]
    earlier = cluster_index[None, :] < cluster_index[:, None]
    before = jnp.sum((same_owner & earlier).astype(jnp.int32), axis=1)
    return owner_map * CL_OWN + before


def masked_weights(left_rows, left_ids, right_rows, right_ids):
    scores = jnp.einsum(
        "id,jd->ij",
        left_rows,
        right_rows,
        preferred_element_type=jnp.float32,
        precision=lax.Precision.HIGHEST,
    )
    linked = (left_ids[:, None] == right_ids[None, :]) & (left_ids[:, None] >= 0)
    return jnp.where(linked, jnp.exp(sharpness * (scores - 1.0)), 0.0)


def tile_sums(left_rows, left_ids, right_rows, right_ids, with_columns):
    right_count = right_rows.shape[0]
    block_rows = 512
    block_count = right_count // block_rows
    right_blocks = right_rows.reshape(block_count, block_rows, right_rows.shape[1])
    id_blocks = right_ids.reshape(block_count, block_rows)

    def one_block(row_total, block_pair):
        weights = masked_weights(left_rows, left_ids, block_pair[0], block_pair[1])
        column_part = jnp.sum(weights, axis=0) if with_columns else None
        return (row_total + jnp.sum(weights, axis=1), column_part)

    row_sums, column_sums = lax.scan(
        one_block, jnp.zeros((left_rows.shape[0],), jnp.float32), (right_blocks, id_blocks)
    )
    if with_columns:
        column_sums = column_sums.reshape(right_count)
    return (row_sums, column_sums)


def local(embeddings, cluster_ids, owner_map, source_order):
    row_count, feature_width = embeddings.shape
    owner_count = lax.axis_size("own")
    capacity = 2 * row_count // owner_count
    slot_count = owner_count * capacity
    cluster_count = owner_map.shape[0]
    unit_embed = unit_rows(embeddings)
    cluster_index = jnp.arange(cluster_count, dtype=jnp.int32)
    cluster_match = cluster_ids[:, None] == cluster_index[None, :]
    row_owner = jnp.sum(jnp.where(cluster_match, owner_map[None, :], 0), axis=1)
    owner_hot = (row_owner[:, None] == jnp.arange(owner_count, dtype=jnp.int32)[None, :]).astype(
        jnp.int32
    )
    rank_index = jnp.sum(jnp.cumsum(owner_hot, axis=0) * owner_hot, axis=1) - 1
    slot_index = row_owner * capacity + rank_index
    send_rows = jnp.zeros((slot_count, feature_width), jnp.float32).at[slot_index].set(unit_embed)
    send_ids = jnp.full((slot_count,), -1, jnp.int32).at[slot_index].set(cluster_ids)
    held_rows, held_ids = (
        lax.all_to_all(
            send_rows.reshape(owner_count, capacity, feature_width),
            "own",
            split_axis=0,
            concat_axis=0,
            tiled=True,
        ),
        lax.all_to_all(
            send_ids.reshape(owner_count, capacity), "own", split_axis=0, concat_axis=0, tiled=True
        ),
    )
    held_rows = held_rows.reshape(slot_count, feature_width)
    held_ids = held_ids.reshape(slot_count)
    group_count = lax.axis_size("grp")
    dup_mass, column_sums = tile_sums(held_rows, held_ids, held_rows, held_ids, False)
    for offset in range(1, group_count // 2 + 1):
        far_rows, far_ids = passed_along((held_rows, held_ids), "grp", -offset)
        returning = offset < group_count - offset
        row_sums, column_sums = tile_sums(held_rows, held_ids, far_rows, far_ids, returning)
        dup_mass = dup_mass + row_sums
        if returning:
            dup_mass = dup_mass + passed_along(column_sums, "grp", offset)
    returned = lax.all_to_all(
        dup_mass.reshape(owner_count, capacity), "own", split_axis=0, concat_axis=0, tiled=True
    )
    row_score = jnp.log(returned.reshape(slot_count)[slot_index])
    dup_score = jnp.zeros((row_count,), jnp.float32).at[source_order].set(row_score)
    position = owner_positions(owner_map)
    position_index = jnp.arange(cluster_count, dtype=jnp.int32)
    ordered = jnp.sum(
        jnp.where(position[None, :] == position_index[:, None], cluster_index[None, :], 0), axis=1
    )
    cluster_hot = (cluster_ids[:, None] == ordered[None, :]).astype(jnp.float32)
    cluster_terms = lax.dot_general(
        cluster_hot,
        unit_embed,
        (((0,), (0,)), ((), ())),
        preferred_element_type=jnp.float32,
        precision=lax.Precision.HIGHEST,
    )
    partial_value = lax.psum_scatter(cluster_terms, "own", scatter_dimension=0, tiled=True)
    cluster_sums = lax.psum(partial_value, "grp")
    centroids = cluster_sums * lax.rsqrt(
        jnp.mean(cluster_sums * cluster_sums, axis=1, keepdims=True) + 1e-06
    )
    return (dup_score, centroids)


def solution(mesh):
    placed = (P(("grp", "own"), None), P(("grp", "own")), P(), P(("grp", "own")))
    return jax.shard_map(
        local,
        mesh=mesh,
        in_specs=placed,
        out_specs=(P(("grp", "own")), P("own", None)),
        check_vma=False,
    )
```

profile of v0, /device:TPU:0, one launch (start us, length us, event | category | flops | bytes accessed | tf_op | source)
XLA Modules:
  0.0 413.7 jit_solution(8130020601397739330)
XLA Ops:
  12.6 9.8 %scatter_custom_fusion.1 = f32[1536,768]{1,0:T(8,128)} fusion(s32[768]{0:T(1024)S(1)} %fusion.42, f32[]{:T(128)} %constant.122.clone.1, f32[768,768]{1,0:T(8,128)S(1)} %copy-done, f32[768]{0:T(1024)S(1)} %add_rsqrt_fusion), kind=kCustom, calls=%fused_computation.40 | custom fusion | flops 589824 | bytes 7081988 | tf_op jit(solution)/shard_map/scatter | solution.py:76
  22.3 6.5 %all-to-all-start.1 = ((f32[8,192,768]{2,1,0:T(8,128)}), f32[8,192,768]{2,1,0:T(8,128)}, u32[]{:S(2)}, u32[]{:S(2)}) async-start(f32[8,192,768]{2,1,0:T(8,128)} %bitcast.91), calls=%async_computation.1 | async-start | bytes 9437184 | tf_op jit(solution)/shard_map/all_to_all | solution.py:79
  29.0 105.1 %all-to-all-done.1 = f32[8,192,768]{2,1,0:T(8,128)} async-done(((f32[8,192,768]{2,1,0:T(8,128)}), f32[8,192,768]{2,1,0:T(8,128)}, u32[]{:S(2)}, u32[]{:S(2)}) %all-to-all-start.1) | async-done | bytes 4718624 | tf_op jit(solution)/shard_map/all_to_all | solution.py:79
  138.6 3.4 scatter_custom_fusion
  146.1 5.5 %all-to-all-done = s32[8,1,192]{2,1,0:T(1,128)S(1)} async-done(((s32[8,1,192]{2,1,0:T(1,128)}), s32[8,1,192]{2,1,0:T(1,128)S(1)}, u32[]{:S(2)}, u32[]{:S(2)}) %all-to-all-start) | async-done | bytes 6176 | tf_op jit(solution)/shard_map/all_to_all | solution.py:86
  153.1 84.7 %collective-permute-done = s32[1536]{0:T(1024)S(1)} collective-permute-done((s32[1536]{0:T(1024)S(1)}, s32[1536]{0:T(1024)S(1)}, u32[]{:S(2)}, u32[]{:S(2)}) %collective-permute-start) | collective-permute-done | bytes 6176 | tf_op jit(solution)/shard_map/ppermute | solution.py:13
  237.8 18.5 %psum.7 = f32[16,768]{1,0:T(8,128)S(1)} all-reduce(f32[16,768]{1,0:T(8,128)} %reduce-scatter.2.cloned.1.call-done), channel_id=1, replica_groups=mesh['grp'=4,'own'=8] {'grp'}, use_global_device_ids=true, to_apply=%region_21.22 | all-reduce | flops 12288 | bytes 98304 | tf_op jit(solution)/shard_map/psum | solution.py:120
  257.0 33.5 %while.44 = (s32[]{:T(128)}, f32[1536]{0:T(1024)S(1)}, s32[8,192]{1,0:T(8,128)}, s32[3,512]{1,0:T(4,128)S(1)}, f32[3,512,768]{2,1,0:T(8,128)}, /*index=5*/f32[15...) while((s32[]{:T(128)}, f32[1536]{0:T(1024)S(1)}, s32[8,192]{1,0:T(8,128)}, ...), condition=%wide.wide.region_9.10_spmd.clone, body=%wide.wide.region_7.9_spmd.clone.sunk | while | flops 7252478976 | bytes 6338155 | solution.py:53
  257.0 11.5 %fusion.67 = f32[1536]{0:T(1024)S(1)} fusion(f32[1536,768]{1,0:T(8,128)} %get-tuple-element.653, f32[3,512,768]{2,1,0:T(8,128)} %get-tuple-element.652, s32[]{:T(128)} %get-tuple-element.639, pred[1536]{0:T(1024)(128)(4,1)S(1)} %broadcast_compare_fusion.9, s32[512]{0:T(512)S(1)} %bitcast.99, s32[1536]{0:T(1024)S(1)} %get-tuple-element.654), kind=kOutput, calls=%fused_computation.11.clone.clone.1 | convolution fusion | flops 7252474368 | bytes 6307840 | tf_op jit(solution)/shard_map/while/body/eval_jaxpr/id,jd->ij/dot_general | solution.py:30
  268.5 10.9 %fusion.67 = f32[1536]{0:T(1024)S(1)} fusion(f32[1536,768]{1,0:T(8,128)} %get-tuple-element.653, f32[3,512,768]{2,1,0:T(8,128)} %get-tuple-element.652, s32[]{:T(128)} %get-tuple-element.639, pred[1536]{0:T(1024)(128)(4,1)S(1)} %broadcast_compare_fusion.9, s32[512]{0:T(512)S(1)} %bitcast.99, s32[1536]{0:T(1024)S(1)} %get-tuple-element.654), kind=kOutput, calls=%fused_computation.11.clone.clone.1 | convolution fusion | flops 7252474368 | bytes 6307840 | tf_op jit(solution)/shard_map/while/body/eval_jaxpr/id,jd->ij/dot_general | solution.py:30
  279.5 10.9 %fusion.67 = f32[1536]{0:T(1024)S(1)} fusion(f32[1536,768]{1,0:T(8,128)} %get-tuple-element.653, f32[3,512,768]{2,1,0:T(8,128)} %get-tuple-element.652, s32[]{:T(128)} %get-tuple-element.639, pred[1536]{0:T(1024)(128)(4,1)S(1)} %broadcast_compare_fusion.9, s32[512]{0:T(512)S(1)} %bitcast.99, s32[1536]{0:T(1024)S(1)} %get-tuple-element.654), kind=kOutput, calls=%fused_computation.11.clone.clone.1 | convolution fusion | flops 7252474368 | bytes 6307840 | tf_op jit(solution)/shard_map/while/body/eval_jaxpr/id,jd->ij/dot_general | solution.py:30
  290.5 32.8 %while.45 = (s32[]{:T(128)}, f32[1536]{0:T(1024)S(1)}, f32[3,512]{1,0:T(4,128)S(1)}, s32[8,192]{1,0:T(8,128)}, s32[3,512]{1,0:T(4,128)S(1)}, /*index=5*/f32[3,51...) while((s32[]{:T(128)}, f32[1536]{0:T(1024)S(1)}, ...), condition=%wide.wide.region_13.14_spmd.clone, body=%wide.wide.region_10.13_spmd.clone.sunk | while | flops 7253264896 | bytes 6344311 | solution.py:53
  290.5 10.8 %fusion.69 = (f32[512]{0:T(512)S(1)}, f32[1536]{0:T(1024)S(1)}) fusion(f32[1536,768]{1,0:T(8,128)} %get-tuple-element.626, f32[3,512,768]{2,1,0:T(8,128)} %get-tuple-element.625, s32[]{:T(128)} %get-tuple-element.610, pred[1536]{0:T(1024)(128)(4,1)S(1)} %broadcast_compare_fusion.10, s32[512]{0:T(512)S(1)} %bitcast.98, ...), kind=kOutput, calls=%fused_computation.78.clone.clone.1 | convolution fusion | flops 7253260288 | bytes 6309888 | tf_op jit(solution)/shard_map/while/body/eval_jaxpr/id,jd->ij/dot_general | solution.py:30
  301.5 10.8 %fusion.69 = (f32[512]{0:T(512)S(1)}, f32[1536]{0:T(1024)S(1)}) fusion(f32[1536,768]{1,0:T(8,128)} %get-tuple-element.626, f32[3,512,768]{2,1,0:T(8,128)} %get-tuple-element.625, s32[]{:T(128)} %get-tuple-element.610, pred[1536]{0:T(1024)(128)(4,1)S(1)} %broadcast_compare_fusion.10, s32[512]{0:T(512)S(1)} %bitcast.98, ...), kind=kOutput, calls=%fused_computation.78.clone.clone.1 | convolution fusion | flops 7253260288 | bytes 6309888 | tf_op jit(solution)/shard_map/while/body/eval_jaxpr/id,jd->ij/dot_general | solution.py:30
  312.4 10.8 %fusion.69 = (f32[512]{0:T(512)S(1)}, f32[1536]{0:T(1024)S(1)}) fusion(f32[1536,768]{1,0:T(8,128)} %get-tuple-element.626, f32[3,512,768]{2,1,0:T(8,128)} %get-tuple-element.625, s32[]{:T(128)} %get-tuple-element.610, pred[1536]{0:T(1024)(128)(4,1)S(1)} %broadcast_compare_fusion.10, s32[512]{0:T(512)S(1)} %bitcast.98, ...), kind=kOutput, calls=%fused_computation.78.clone.clone.1 | convolution fusion | flops 7253260288 | bytes 6309888 | tf_op jit(solution)/shard_map/while/body/eval_jaxpr/id,jd->ij/dot_general | solution.py:30
  323.6 32.1 %collective-permute-done.4 = f32[1536,768]{1,0:T(8,128)} collective-permute-done((f32[1536,768]{1,0:T(8,128)}, f32[1536,768]{1,0:T(8,128)}, u32[]{:S(2)}, u32[]{:S(2)}) %collective-permute-start.4) | collective-permute-done | bytes 4718624 | tf_op jit(solution)/shard_map/ppermute | solution.py:13
  355.8 32.9 %while.46 = (s32[]{:T(128)}, f32[1536]{0:T(1024)S(1)}, s32[8,192]{1,0:T(8,128)}, s32[3,512]{1,0:T(4,128)S(1)}, f32[3,512,768]{2,1,0:T(8,128)}, /*index=5*/f32[15...) while((s32[]{:T(128)}, f32[1536]{0:T(1024)S(1)}, s32[8,192]{1,0:T(8,128)}, ...), condition=%wide.wide.region_16.17_spmd.clone, body=%wide.wide.region_14.16_spmd.clone.sunk | while | flops 7252478976 | bytes 6338155 | solution.py:53
  355.8 10.9 %fusion.72 = f32[1536]{0:T(1024)S(1)} fusion(f32[1536,768]{1,0:T(8,128)} %get-tuple-element.596, f32[3,512,768]{2,1,0:T(8,128)} %get-tuple-element.595, s32[]{:T(128)} %get-tuple-element.582, pred[1536]{0:T(1024)(128)(4,1)S(1)} %broadcast_compare_fusion.11, s32[512]{0:T(512)S(1)} %bitcast.100, s32[1536]{0:T(1024)S(1)} %get-tuple-element.597), kind=kOutput, calls=%fused_computation.34.clone.clone.1 | convolution fusion | flops 7252474368 | bytes 6307840 | tf_op jit(solution)/shard_map/while/body/eval_jaxpr/id,jd->ij/dot_general | solution.py:30
  366.7 10.9 %fusion.72 = f32[1536]{0:T(1024)S(1)} fusion(f32[1536,768]{1,0:T(8,128)} %get-tuple-element.596, f32[3,512,768]{2,1,0:T(8,128)} %get-tuple-element.595, s32[]{:T(128)} %get-tuple-element.582, pred[1536]{0:T(1024)(128)(4,1)S(1)} %broadcast_compare_fusion.11, s32[512]{0:T(512)S(1)} %bitcast.100, s32[1536]{0:T(1024)S(1)} %get-tuple-element.597), kind=kOutput, calls=%fused_computation.34.clone.clone.1 | convolution fusion | flops 7252474368 | bytes 6307840 | tf_op jit(solution)/shard_map/while/body/eval_jaxpr/id,jd->ij/dot_general | solution.py:30
  377.7 10.9 %fusion.72 = f32[1536]{0:T(1024)S(1)} fusion(f32[1536,768]{1,0:T(8,128)} %get-tuple-element.596, f32[3,512,768]{2,1,0:T(8,128)} %get-tuple-element.595, s32[]{:T(128)} %get-tuple-element.582, pred[1536]{0:T(1024)(128)(4,1)S(1)} %broadcast_compare_fusion.11, s32[512]{0:T(512)S(1)} %bitcast.100, s32[1536]{0:T(1024)S(1)} %get-tuple-element.597), kind=kOutput, calls=%fused_computation.34.clone.clone.1 | convolution fusion | flops 7252474368 | bytes 6307840 | tf_op jit(solution)/shard_map/while/body/eval_jaxpr/id,jd->ij/dot_general | solution.py:30
  389.4 3.4 all-to-all-start.2
  393.4 4.9 %all-to-all-done.2 = f32[8,1,192]{2,1,0:T(1,128)S(1)} async-done(((f32[8,1,192]{2,1,0:T(1,128)}), f32[8,1,192]{2,1,0:T(1,128)S(1)}, u32[]{:S(2)}, u32[]{:S(2)}) %all-to-all-start.2) | async-done | bytes 6176 | tf_op jit(solution)/shard_map/all_to_all | solution.py:101
  398.4 4.5 %gather_fusion = f32[768]{0:T(1024)S(1)} fusion(f32[1536]{0:T(1024)S(1)} %reshape.150, s32[1024]{0:T(1024)S(1)} %pad_clamp_fusion), kind=kCustom, calls=%fused_computation | custom fusion | bytes 9216 | tf_op jit(solution)/shard_map/gather | solution.py:104
  402.9 3.9 scatter_custom_fusion.2
  (93 shorter events, 18.3 us)
Async XLA Ops:
  7.2 5.4 %copy-start = (f32[768,768]{1,0:T(8,128)S(1)}, f32[768,768]{1,0:T(8,128)}, u32[]{:S(2)}) copy-start(f32[768,768]{1,0:T(8,128)} %param.10) | copy-start | bytes 7077892
  22.3 6.5 %copy-start.4 = (s32[128]{0:T(128)S(1)}, s32[128]{0:T(128)}, u32[]{:S(2)}) copy-start(s32[128]{0:T(128)} %param.12) | copy-start | bytes 1540
  22.3 114.4 %copy-start.2 = (s32[768]{0:T(1024)S(1)}, s32[768]{0:T(1024)}, u32[]{:S(2)}) copy-start(s32[768]{0:T(1024)} %param.11) | copy-start | bytes 9220
  22.3 111.8 %all-to-all-start.1 = ((f32[8,192,768]{2,1,0:T(8,128)}), f32[8,192,768]{2,1,0:T(8,128)}, u32[]{:S(2)}, u32[]{:S(2)}) async-start(f32[8,192,768]{2,1,0:T(8,128)} %bitcast.91), calls=%async_computation.1 | async-start | bytes 9437184 | tf_op jit(solution)/shard_map/all_to_all | solution.py:79
  28.8 117.3 %copy-start.3 = (s32[768]{0:T(1024)S(1)}, s32[768]{0:T(1024)}, u32[]{:S(2)}) copy-start(s32[768]{0:T(1024)} %param.13) | copy-start | bytes 9220
  28.8 209.0 %reduce-scatter.2.cloned.1.call-start = ((), (), s32[]{:S(2)}) async-start(), calls=%async_computation.4 | async-start | bytes 442368 | tf_op jit(solution)/shard_map/reduce_scatter | solution.py:119
  134.1 156.3 %collective-permute-start.1 = (f32[1536,768]{1,0:T(8,128)}, f32[1536,768]{1,0:T(8,128)}, u32[]{:S(2)}, u32[]{:S(2)}) collective-permute-start(f32[1536,768]{1,0:T(8,128)} %bitcast.6), channel_id=1, source_target_pairs={{0,24},{8,0},{16,8},{24,16},{1,25},{9,1},{17,9},{25,17},{2,26},{10... | collective-permute-start | bytes 14155784 | tf_op jit(solution)/shard_map/ppermute | solution.py:13
  142.7 8.9 %all-to-all-start = ((s32[8,1,192]{2,1,0:T(1,128)}), s32[8,1,192]{2,1,0:T(1,128)S(1)}, u32[]{:S(2)}, u32[]{:S(2)}) async-start(s32[8,1,192]{2,1,0:T(1,128)} %all_to_all.17), calls=%async_computation | async-start | bytes 16384 | tf_op jit(solution)/shard_map/all_to_all | solution.py:86
  151.7 86.1 %collective-permute-start = (s32[1536]{0:T(1024)S(1)}, s32[1536]{0:T(1024)S(1)}, u32[]{:S(2)}, u32[]{:S(2)}) collective-permute-start(s32[1536]{0:T(1024)S(1)} %reshape.144), channel_id=1, source_target_pairs={{0,24},{8,0},{16,8},{24,16},{1,25},{9,1},{17,9},{25,17},{2,26},{10... | collective-permute-start | bytes 18440 | tf_op jit(solution)/shard_map/ppermute | solution.py:13
  152.2 85.6 %collective-permute-start.3 = (s32[1536]{0:T(1024)S(1)}, s32[1536]{0:T(1024)S(1)}, u32[]{:S(2)}, u32[]{:S(2)}) collective-permute-start(s32[1536]{0:T(1024)S(1)} %reshape.144), channel_id=1, source_target_pairs={{0,16},{8,24},{16,0},{24,8},{1,17},{9,25},{17,1},{25,9},{2,18},{10... | collective-permute-start | bytes 18440 | tf_op jit(solution)/shard_map/ppermute | solution.py:13
  152.8 104.2 %copy-start.1 = (s32[8,1,192]{2,0,1:T(8,128)}, s32[8,1,192]{2,0,1:T(8,128)S(1)}, u32[]{:S(2)}) copy-start(s32[8,1,192]{2,0,1:T(8,128)S(1)} %copy.16) | copy-start | bytes 18436
  256.4 99.3 %collective-permute-start.4 = (f32[1536,768]{1,0:T(8,128)}, f32[1536,768]{1,0:T(8,128)}, u32[]{:S(2)}, u32[]{:S(2)}) collective-permute-start(f32[1536,768]{1,0:T(8,128)} %bitcast.6), channel_id=1, source_target_pairs={{0,16},{8,24},{16,0},{24,8},{1,17},{9,25},{17,1},{25,9},{2,18},{10... | collective-permute-start | bytes 14155784 | tf_op jit(solution)/shard_map/ppermute | solution.py:13
  323.3 65.3 %collective-permute-start.2 = (f32[1536]{0:T(1024)S(1)}, f32[1536]{0:T(1024)S(1)}, u32[]{:S(2)}, u32[]{:S(2)}) collective-permute-start(f32[1536]{0:T(1024)S(1)} %reshape.147), channel_id=1, source_target_pairs={{0,8},{8,16},{16,24},{24,0},{1,9},{9,17},{17,25},{25,1},{2,10},{10... | collective-permute-start | bytes 18440 | tf_op jit(solution)/shard_map/ppermute | solution.py:13
  389.4 9.0 %all-to-all-start.2 = ((f32[8,1,192]{2,1,0:T(1,128)}), f32[8,1,192]{2,1,0:T(1,128)S(1)}, u32[]{:S(2)}, u32[]{:S(2)}) async-start(f32[8,1,192]{2,1,0:T(1,128)} %all_to_all.21), calls=%async_computation.2 | async-start | bytes 16384 | tf_op jit(solution)/shard_map/all_to_all | solution.py:101
Sparse Core Ops, SparseCore 0:
  138.8 28.2 reduce-scatter.1
where the time goes:
time: 414 us
  waiting for transfers between devices  232 us (56%)
  matrix products  100 us (24%)
  blocking collectives  18.5 us (4%)
  starting transfers between devices  17.5 us (4%)
  other arithmetic  16.1 us (4%)
  between operations  14.3 us (3%)
  local copies, waits for them, and re-layouts  14.2 us (3%)
    ppermute x5, waiting for transfers between devices, passed_along(): return lax.ppermute(value, axis, pairs)  117 us
    all_to_all x1, waiting for transfers between devices, local(): lax.all_to_all(send_rows.reshape(owner_count, capacity, feature_width), '...  105 us
    dot_general x9, matrix products, masked_weights(): jnp.einsum('id,jd->ij', left_rows, right_rows, preferred_element_type=jnp...  98.5 us
    psum x1, blocking collectives, local(): cluster_sums = lax.psum(partial_value, 'grp')  18.5 us
    scatter x1, other arithmetic, local(): jnp.zeros((slot_count, feature_width), jnp.float32).at[slot_index]  9.76 us
  transfers between devices with their start and end apart: 9, of which 5 were waited for; matrix products, arithmetic and copies ran while one was open for 26% of the time, Pallas kernels for 0%

commit v1 on v0

--- a/solution.py
+++ b/solution.py
@@ -5,6 +5,29 @@
 
 CL_OWN = 16
 sharpness = 6.0
+
+
+def in_blocks(x, dim, devices):
+    before, after = (x.shape[:dim], x.shape[dim + 1 :])
+    return jnp.moveaxis(x.reshape(*before, devices, -1, *after), dim, 0)
+
+
+def joined_along(pieces, dim):
+    pieces = jnp.moveaxis(pieces, 0, dim)
+    dims = pieces.shape
+    return pieces.reshape(*dims[:dim], dims[dim] * dims[dim + 1], *dims[dim + 2 :])
+
+
+def rotated_exchange(array, axis, split_dim, concat_dim):
+    size, place = (lax.axis_size(axis), lax.axis_index(axis))
+    blocks = in_blocks(array, split_dim, size)
+    result = blocks
+    for lap in range(1, size):
+        target, source = ((place + lap) % size, (place - lap) % size)
+        sent = lax.dynamic_index_in_dim(blocks, target, 0)
+        other = lax.ppermute(sent, axis, [(i, (i + lap) % size) for i in range(size)])
+        result = lax.dynamic_update_slice_in_dim(result, other, source, axis=0)
+    return joined_along(result, concat_dim)
 
 
 def passed_along(value, axis, steps):
@@ -76,13 +99,7 @@
     send_rows = jnp.zeros((slot_count, feature_width), jnp.float32).at[slot_index].set(unit_embed)
     send_ids = jnp.full((slot_count,), -1, jnp.int32).at[slot_index].set(cluster_ids)
     held_rows, held_ids = (
-        lax.all_to_all(
-            send_rows.reshape(owner_count, capacity, feature_width),
-            "own",
-            split_axis=0,
-            concat_axis=0,
-            tiled=True,
-        ),
+        rotated_exchange(send_rows.reshape(owner_count, capacity, feature_width), "own", 0, 0),
         lax.all_to_all(
             send_ids.reshape(owner_count, capacity), "own", split_axis=0, concat_axis=0, tiled=True
         ),

time: 414 us -> 418 us (level)
  waiting for transfers between devices: 232 us -> 159 us
  starting transfers between devices: 17.5 us -> 73.8 us
  local copies, waits for them, and re-layouts: 14.2 us -> 28.5 us
  blocking collectives: 18.5 us -> 24.8 us
    all_to_all x1 -> x0, waiting for transfers between devices: 105 us -> none  [local(): lax.all_to_all(send_rows.reshape(owner_count, capacity, feature_width), '...]
    ppermute x0 -> x7, waiting for transfers between devices: none -> 65.6 us  [rotated_exchange(): lax.ppermute(sent, axis, [(i, (i + lap) % size) for i in range(size)])]
    ppermute x5, waiting for transfers between devices: 117 us -> 83.2 us  [passed_along(): return lax.ppermute(value, axis, pairs)]
    all_to_all x1, starting transfers between devices: 3.33 us -> 32.9 us  [local(): lax.all_to_all(send_ids.reshape(owner_count, capacity), 'own', split_axis...]
    all_to_all x1, starting transfers between devices: 3.36 us -> 29.4 us  [local(): lax.all_to_all(dup_mass.reshape(owner_count, capacity), 'own', split_axis...]
    dynamic_update_slice x0 -> x6, local copies, waits for them, and re-layouts: none -> 9.46 us  [rotated_exchange(): result = lax.dynamic_update_slice_in_dim(result, other, source, axis=0)]
    ppermute x0 -> x7, starting transfers between devices: none -> 7.14 us  [rotated_exchange(): lax.ppermute(sent, axis, [(i, (i + lap) % size) for i in range(size)])]
    all_to_all x1 -> x0, starting transfers between devices: 6.49 us -> none  [local(): lax.all_to_all(send_rows.reshape(owner_count, capacity, feature_width), '...]
  transfers between devices with their start and end apart: 9 -> 15, of which waited for: 5 -> 8; matrix products, arithmetic and copies ran while one was open for 26% -> 27% of each run, Pallas kernels for 0% -> 0%
where the time goes in v1:
time: 418 us
  waiting for transfers between devices  159 us (38%)
  matrix products  100 us (24%)
  starting transfers between devices  73.8 us (18%)
  local copies, waits for them, and re-layouts  28.5 us (7%)
  blocking collectives  24.8 us (6%)
  other arithmetic  16.1 us (4%)
  between operations  14.3 us (3%)
    dot_general x9, matrix products, masked_weights(): jnp.einsum('id,jd->ij', left_rows, right_rows, preferred_element_type=jnp...  98.4 us
    ppermute x5, waiting for transfers between devices, passed_along(): return lax.ppermute(value, axis, pairs)  83.2 us
    ppermute x7, waiting for transfers between devices, rotated_exchange(): lax.ppermute(sent, axis, [(i, (i + lap) % size) for i in range(size)])  65.6 us
    all_to_all x1, starting transfers between devices, local(): lax.all_to_all(send_ids.reshape(owner_count, capacity), 'own', split_axis...  32.9 us
    all_to_all x1, starting transfers between devices, local(): lax.all_to_all(dup_mass.reshape(owner_count, capacity), 'own', split_axis...  29.4 us
    psum x1, blocking collectives, local(): cluster_sums = lax.psum(partial_value, 'grp')  24.8 us
    scatter x1, other arithmetic, local(): jnp.zeros((slot_count, feature_width), jnp.float32).at[slot_index]  9.83 us
    dynamic_update_slice x6, local copies, waits for them, and re-layouts, rotated_exchange(): result = lax.dynamic_update_slice_in_dim(result, other, source, axis=0)  9.46 us
  transfers between devices with their start and end apart: 15, of which 8 were waited for; matrix products, arithmetic and copies ran while one was open for 27% of the time, Pallas kernels for 0%

profile of v1, /device:TPU:0, one launch (start us, length us, event | category | flops | bytes accessed | tf_op | source)
XLA Modules:
  0.0 417.6 jit_solution(9799029502894822161)
XLA Ops:
  12.6 9.8 %scatter_custom_fusion.1 = f32[1536,768]{1,0:T(8,128)} fusion(s32[768]{0:T(1024)S(1)} %fusion.42, f32[]{:T(128)} %constant.217.clone.1, f32[768,768]{1,0:T(8,128)S(1)} %copy-done, f32[768]{0:T(1024)S(1)} %add_rsqrt_fusion), kind=kCustom, calls=%fused_computation.40 | custom fusion | flops 589824 | bytes 7081988 | tf_op jit(solution)/shard_map/scatter | solution.py:99
  24.1 11.7 %collective-permute-done = f32[1,1,192,768]{3,2,0,1:T(8,128)} collective-permute-done((f32[1,1,192,768]{3,2,0,1:T(8,128)S(1)}, f32[1,1,192,768]{3,2,0,1:T(8,128)}, u32[]{:S(2)}, u32[]{:S(2)}) %collective-permute-start) | collective-permute-done | bytes 589856 | tf_op jit(solution)/shard_map/ppermute | solution.py:28
  46.3 11.7 %collective-permute-done.1 = f32[1,1,192,768]{3,2,0,1:T(8,128)} collective-permute-done((f32[1,1,192,768]{3,2,0,1:T(8,128)}, f32[1,1,192,768]{3,2,0,1:T(8,128)}, u32[]{:S(2)}, u32[]{:S(2)}) %collective-permute-start.1) | collective-permute-done | bytes 589856 | tf_op jit(solution)/shard_map/ppermute | solution.py:28
  60.0 39.0 %collective-permute-done.2 = f32[1,1,192,768]{3,2,0,1:T(8,128)} collective-permute-done((f32[1,1,192,768]{3,2,0,1:T(8,128)}, f32[1,1,192,768]{3,2,0,1:T(8,128)}, u32[]{:S(2)}, u32[]{:S(2)}) %collective-permute-start.2) | collective-permute-done | bytes 589856 | tf_op jit(solution)/shard_map/ppermute | solution.py:28
  118.3 32.9 %all-to-all-start = ((s32[8,1,192]{2,1,0:T(1,128)}), s32[8,1,192]{2,1,0:T(1,128)S(1)}, u32[]{:S(2)}, u32[]{:S(2)}) async-start(s32[8,1,192]{2,1,0:T(1,128)} %all_to_all.14), calls=%async_computation | async-start | bytes 16384 | tf_op jit(solution)/shard_map/all_to_all | solution.py:103
  151.3 5.6 %all-to-all-done = s32[8,1,192]{2,1,0:T(1,128)S(1)} async-done(((s32[8,1,192]{2,1,0:T(1,128)}), s32[8,1,192]{2,1,0:T(1,128)S(1)}, u32[]{:S(2)}, u32[]{:S(2)}) %all-to-all-start) | async-done | bytes 6176 | tf_op jit(solution)/shard_map/all_to_all | solution.py:103
  158.3 50.1 %collective-permute-done.7 = s32[1536]{0:T(1024)S(1)} collective-permute-done((s32[1536]{0:T(1024)S(1)}, s32[1536]{0:T(1024)S(1)}, u32[]{:S(2)}, u32[]{:S(2)}) %collective-permute-start.7) | collective-permute-done | bytes 6176 | tf_op jit(solution)/shard_map/ppermute | solution.py:36
  208.5 24.8 %psum.7 = f32[16,768]{1,0:T(8,128)S(1)} all-reduce(f32[16,768]{1,0:T(8,128)} %reduce-scatter.2.cloned.1.call-done), channel_id=1, replica_groups=mesh['grp'=4,'own'=8] {'grp'}, use_global_device_ids=true, to_apply=%region_21.22 | all-reduce | flops 12288 | bytes 98304 | tf_op jit(solution)/shard_map/psum | solution.py:137
  234.0 33.4 %while.44 = (s32[]{:T(128)}, f32[1536]{0:T(1024)S(1)}, s32[8,192]{1,0:T(8,128)}, s32[3,512]{1,0:T(4,128)S(1)}, f32[3,512,768]{2,1,0:T(8,128)}, /*index=5*/f32[15...) while((s32[]{:T(128)}, f32[1536]{0:T(1024)S(1)}, s32[8,192]{1,0:T(8,128)}, ...), condition=%wide.wide.region_9.10_spmd.clone, body=%wide.wide.region_7.9_spmd.clone.sunk | while | flops 7252478976 | bytes 6338155 | solution.py:76
  234.0 11.4 %fusion.67 = f32[1536]{0:T(1024)S(1)} fusion(f32[1536,768]{1,0:T(8,128)} %get-tuple-element.660, f32[3,512,768]{2,1,0:T(8,128)} %bitcast.97, s32[]{:T(128)} %get-tuple-element.646, pred[1536]{0:T(1024)(128)(4,1)S(1)} %broadcast_compare_fusion.9, s32[512]{0:T(512)S(1)} %bitcast.106, s32[1536]{0:T(1024)S(1)} %get-tuple-element.661), kind=kOutput, calls=%fused_computation.11.clone.clone.1 | convolution fusion | flops 7252474368 | bytes 6307840 | tf_op jit(solution)/shard_map/while/body/eval_jaxpr/id,jd->ij/dot_general | solution.py:53
  245.5 10.9 %fusion.67 = f32[1536]{0:T(1024)S(1)} fusion(f32[1536,768]{1,0:T(8,128)} %get-tuple-element.660, f32[3,512,768]{2,1,0:T(8,128)} %bitcast.97, s32[]{:T(128)} %get-tuple-element.646, pred[1536]{0:T(1024)(128)(4,1)S(1)} %broadcast_compare_fusion.9, s32[512]{0:T(512)S(1)} %bitcast.106, s32[1536]{0:T(1024)S(1)} %get-tuple-element.661), kind=kOutput, calls=%fused_computation.11.clone.clone.1 | convolution fusion | flops 7252474368 | bytes 6307840 | tf_op jit(solution)/shard_map/while/body/eval_jaxpr/id,jd->ij/dot_general | solution.py:53
  256.5 10.9 %fusion.67 = f32[1536]{0:T(1024)S(1)} fusion(f32[1536,768]{1,0:T(8,128)} %get-tuple-element.660, f32[3,512,768]{2,1,0:T(8,128)} %bitcast.97, s32[]{:T(128)} %get-tuple-element.646, pred[1536]{0:T(1024)(128)(4,1)S(1)} %broadcast_compare_fusion.9, s32[512]{0:T(512)S(1)} %bitcast.106, s32[1536]{0:T(1024)S(1)} %get-tuple-element.661), kind=kOutput, calls=%fused_computation.11.clone.clone.1 | convolution fusion | flops 7252474368 | bytes 6307840 | tf_op jit(solution)/shard_map/while/body/eval_jaxpr/id,jd->ij/dot_general | solution.py:53
  267.4 32.8 %while.45 = (s32[]{:T(128)}, f32[1536]{0:T(1024)S(1)}, f32[3,512]{1,0:T(4,128)S(1)}, s32[8,192]{1,0:T(8,128)}, s32[3,512]{1,0:T(4,128)S(1)}, /*index=5*/f32[3,51...) while((s32[]{:T(128)}, f32[1536]{0:T(1024)S(1)}, ...), condition=%wide.wide.region_13.14_spmd.clone, body=%wide.wide.region_10.13_spmd.clone.sunk | while | flops 7253264896 | bytes 6344311 | solution.py:76
  267.5 10.8 %fusion.69 = (f32[512]{0:T(512)S(1)}, f32[1536]{0:T(1024)S(1)}) fusion(f32[1536,768]{1,0:T(8,128)} %get-tuple-element.633, f32[3,512,768]{2,1,0:T(8,128)} %get-tuple-element.632, s32[]{:T(128)} %get-tuple-element.617, pred[1536]{0:T(1024)(128)(4,1)S(1)} %broadcast_compare_fusion.10, s32[512]{0:T(512)S(1)} %bitcast.105, ...), kind=kOutput, calls=%fused_computation.92.clone.clone.1 | convolution fusion | flops 7253260288 | bytes 6309888 | tf_op jit(solution)/shard_map/while/body/eval_jaxpr/id,jd->ij/dot_general | solution.py:53
  278.4 10.8 %fusion.69 = (f32[512]{0:T(512)S(1)}, f32[1536]{0:T(1024)S(1)}) fusion(f32[1536,768]{1,0:T(8,128)} %get-tuple-element.633, f32[3,512,768]{2,1,0:T(8,128)} %get-tuple-element.632, s32[]{:T(128)} %get-tuple-element.617, pred[1536]{0:T(1024)(128)(4,1)S(1)} %broadcast_compare_fusion.10, s32[512]{0:T(512)S(1)} %bitcast.105, ...), kind=kOutput, calls=%fused_computation.92.clone.clone.1 | convolution fusion | flops 7253260288 | bytes 6309888 | tf_op jit(solution)/shard_map/while/body/eval_jaxpr/id,jd->ij/dot_general | solution.py:53
  289.3 10.8 %fusion.69 = (f32[512]{0:T(512)S(1)}, f32[1536]{0:T(1024)S(1)}) fusion(f32[1536,768]{1,0:T(8,128)} %get-tuple-element.633, f32[3,512,768]{2,1,0:T(8,128)} %get-tuple-element.632, s32[]{:T(128)} %get-tuple-element.617, pred[1536]{0:T(1024)(128)(4,1)S(1)} %broadcast_compare_fusion.10, s32[512]{0:T(512)S(1)} %bitcast.105, ...), kind=kOutput, calls=%fused_computation.92.clone.clone.1 | convolution fusion | flops 7253260288 | bytes 6309888 | tf_op jit(solution)/shard_map/while/body/eval_jaxpr/id,jd->ij/dot_general | solution.py:53
  300.5 33.1 %collective-permute-done.11 = f32[1536,768]{1,0:T(8,128)} collective-permute-done((f32[1536,768]{1,0:T(8,128)}, f32[1536,768]{1,0:T(8,128)}, u32[]{:S(2)}, u32[]{:S(2)}) %collective-permute-start.11) | collective-permute-done | bytes 4718624 | tf_op jit(solution)/shard_map/ppermute | solution.py:36
  333.6 32.9 %while.46 = (s32[]{:T(128)}, f32[1536]{0:T(1024)S(1)}, s32[8,192]{1,0:T(8,128)}, s32[3,512]{1,0:T(4,128)S(1)}, f32[3,512,768]{2,1,0:T(8,128)}, /*index=5*/f32[15...) while((s32[]{:T(128)}, f32[1536]{0:T(1024)S(1)}, s32[8,192]{1,0:T(8,128)}, ...), condition=%wide.wide.region_16.17_spmd.clone, body=%wide.wide.region_14.16_spmd.clone.sunk | while | flops 7252478976 | bytes 6338155 | solution.py:76
  333.6 10.9 %fusion.72 = f32[1536]{0:T(1024)S(1)} fusion(f32[1536,768]{1,0:T(8,128)} %get-tuple-element.603, f32[3,512,768]{2,1,0:T(8,128)} %get-tuple-element.602, s32[]{:T(128)} %get-tuple-element.589, pred[1536]{0:T(1024)(128)(4,1)S(1)} %broadcast_compare_fusion.11, s32[512]{0:T(512)S(1)} %bitcast.107, s32[1536]{0:T(1024)S(1)} %get-tuple-element.604), kind=kOutput, calls=%fused_computation.34.clone.clone.1 | convolution fusion | flops 7252474368 | bytes 6307840 | tf_op jit(solution)/shard_map/while/body/eval_jaxpr/id,jd->ij/dot_general | solution.py:53
  344.6 10.9 %fusion.72 = f32[1536]{0:T(1024)S(1)} fusion(f32[1536,768]{1,0:T(8,128)} %get-tuple-element.603, f32[3,512,768]{2,1,0:T(8,128)} %get-tuple-element.602, s32[]{:T(128)} %get-tuple-element.589, pred[1536]{0:T(1024)(128)(4,1)S(1)} %broadcast_compare_fusion.11, s32[512]{0:T(512)S(1)} %bitcast.107, s32[1536]{0:T(1024)S(1)} %get-tuple-element.604), kind=kOutput, calls=%fused_computation.34.clone.clone.1 | convolution fusion | flops 7252474368 | bytes 6307840 | tf_op jit(solution)/shard_map/while/body/eval_jaxpr/id,jd->ij/dot_general | solution.py:53
  355.6 10.9 %fusion.72 = f32[1536]{0:T(1024)S(1)} fusion(f32[1536,768]{1,0:T(8,128)} %get-tuple-element.603, f32[3,512,768]{2,1,0:T(8,128)} %get-tuple-element.602, s32[]{:T(128)} %get-tuple-element.589, pred[1536]{0:T(1024)(128)(4,1)S(1)} %broadcast_compare_fusion.11, s32[512]{0:T(512)S(1)} %bitcast.107, s32[1536]{0:T(1024)S(1)} %get-tuple-element.604), kind=kOutput, calls=%fused_computation.34.clone.clone.1 | convolution fusion | flops 7252474368 | bytes 6307840 | tf_op jit(solution)/shard_map/while/body/eval_jaxpr/id,jd->ij/dot_general | solution.py:53
  367.2 29.4 %all-to-all-start.1 = ((f32[8,1,192]{2,1,0:T(1,128)}), f32[8,1,192]{2,1,0:T(1,128)S(1)}, u32[]{:S(2)}, u32[]{:S(2)}) async-start(f32[8,1,192]{2,1,0:T(1,128)} %all_to_all.17), calls=%async_computation.1 | async-start | bytes 16384 | tf_op jit(solution)/shard_map/all_to_all | solution.py:118
  397.3 4.9 %all-to-all-done.1 = f32[8,1,192]{2,1,0:T(1,128)S(1)} async-done(((f32[8,1,192]{2,1,0:T(1,128)}), f32[8,1,192]{2,1,0:T(1,128)S(1)}, u32[]{:S(2)}, u32[]{:S(2)}) %all-to-all-start.1) | async-done | bytes 6176 | tf_op jit(solution)/shard_map/all_to_all | solution.py:118
  402.3 4.5 %gather_fusion = f32[768]{0:T(1024)S(1)} fusion(f32[1536]{0:T(1024)S(1)} %reshape.142, s32[1024]{0:T(1024)S(1)} %pad_clamp_fusion), kind=kCustom, calls=%fused_computation | custom fusion | bytes 9216 | tf_op jit(solution)/shard_map/gather | solution.py:121
  (115 shorter events, 47.0 us)
Async XLA Ops:
  7.2 5.4 %copy-start = (f32[768,768]{1,0:T(8,128)S(1)}, f32[768,768]{1,0:T(8,128)}, u32[]{:S(2)}) copy-start(f32[768,768]{1,0:T(8,128)} %param.10) | copy-start | bytes 7077892
  7.2 201.3 %reduce-scatter.2.cloned.1.call-start = ((), (), s32[]{:S(2)}) async-start(), calls=%async_computation.3 | async-start | bytes 442368 | tf_op jit(solution)/shard_map/reduce_scatter | solution.py:136
  23.6 12.2 %collective-permute-start = (f32[1,1,192,768]{3,2,0,1:T(8,128)S(1)}, f32[1,1,192,768]{3,2,0,1:T(8,128)}, u32[]{:S(2)}, u32[]{:S(2)}) collective-permute-start(f32[1,1,192,768]{3,2,0,1:T(8,128)S(1)} %constant_dynamic-slice_fusion.9), channel_id=1, source_target_pairs={{0,1},{1,2},{2,3},{3,4},{4,5},{5,6},{6,7},{7,0},{8,9},{9,10},{10,1... | collective-permute-start | bytes 1769480 | tf_op jit(solution)/shard_map/ppermute | solution.py:28
  24.1 22.0 %copy-start.4 = (s32[128]{0:T(128)S(1)}, s32[128]{0:T(128)}, u32[]{:S(2)}) copy-start(s32[128]{0:T(128)} %param.12) | copy-start | bytes 1540
  39.5 18.5 %collective-permute-start.1 = (f32[1,1,192,768]{3,2,0,1:T(8,128)}, f32[1,1,192,768]{3,2,0,1:T(8,128)}, u32[]{:S(2)}, u32[]{:S(2)}) collective-permute-start(f32[1,1,192,768]{3,2,0,1:T(8,128)} %get-tuple-element.361), channel_id=1, source_target_pairs={{0,2},{1,3},{2,4},{3,5},{4,6},{5,7},{6,0},{7,1},{8,10},{9,11},{10,... | collective-permute-start | bytes 1769480 | tf_op jit(solution)/shard_map/ppermute | solution.py:28
  39.8 59.1 %collective-permute-start.2 = (f32[1,1,192,768]{3,2,0,1:T(8,128)}, f32[1,1,192,768]{3,2,0,1:T(8,128)}, u32[]{:S(2)}, u32[]{:S(2)}) collective-permute-start(f32[1,1,192,768]{3,2,0,1:T(8,128)} %get-tuple-element.360), channel_id=1, source_target_pairs={{0,3},{1,4},{2,5},{3,6},{4,7},{5,0},{6,1},{7,2},{8,11},{9,12},{10,... | collective-permute-start | bytes 1769480 | tf_op jit(solution)/shard_map/ppermute | solution.py:28
  39.9 61.0 %collective-permute-start.3 = (f32[1,1,192,768]{3,2,0,1:T(8,128)}, f32[1,1,192,768]{3,2,0,1:T(8,128)}, u32[]{:S(2)}, u32[]{:S(2)}) collective-permute-start(f32[1,1,192,768]{3,2,0,1:T(8,128)} %get-tuple-element.359), channel_id=1, source_target_pairs={{0,4},{1,5},{2,6},{3,7},{4,0},{5,1},{6,2},{7,3},{8,12},{9,13},{10,... | collective-permute-start | bytes 1769480 | tf_op jit(solution)/shard_map/ppermute | solution.py:28
  42.4 60.4 %collective-permute-start.4 = (f32[1,1,192,768]{3,2,0,1:T(8,128)}, f32[1,1,192,768]{3,2,0,1:T(8,128)}, u32[]{:S(2)}, u32[]{:S(2)}) collective-permute-start(f32[1,1,192,768]{3,2,0,1:T(8,128)} %get-tuple-element.358), channel_id=1, source_target_pairs={{0,5},{1,6},{2,7},{3,0},{4,1},{5,2},{6,3},{7,4},{8,13},{9,14},{10,... | collective-permute-start | bytes 1769480 | tf_op jit(solution)/shard_map/ppermute | solution.py:28
  44.8 59.9 %collective-permute-start.5 = (f32[1,1,192,768]{3,2,0,1:T(8,128)S(1)}, f32[1,1,192,768]{3,2,0,1:T(8,128)S(1)}, u32[]{:S(2)}, u32[]{:S(2)}) collective-permute-start(f32[1,1,192,768]{3,2,0,1:T(8,128)S(1)} %get-tuple-element.357), channel_id=1, source_target_pairs={{0,6},{1,7},{2,0},{3,1},{4,2},{5,3},{6,4},{7,5},{8,14},{9,15},{10,... | collective-permute-start | bytes 1769480 | tf_op jit(solution)/shard_map/ppermute | solution.py:28
  58.0 50.9 %collective-permute-start.6 = (f32[1,1,192,768]{3,2,0,1:T(8,128)S(1)}, f32[1,1,192,768]{3,2,0,1:T(8,128)S(1)}, u32[]{:S(2)}, u32[]{:S(2)}) collective-permute-start(f32[1,1,192,768]{3,2,0,1:T(8,128)S(1)} %get-tuple-element.356), channel_id=1, source_target_pairs={{0,7},{1,0},{2,1},{3,2},{4,3},{5,4},{6,5},{7,6},{8,15},{9,8},{10,9... | collective-permute-start | bytes 1769480 | tf_op jit(solution)/shard_map/ppermute | solution.py:28
  60.0 52.2 %copy-start.5 = (s32[128]{0:T(128)S(1)}, s32[128]{0:T(128)}, u32[]{:S(2)}) copy-start(s32[128]{0:T(128)} %param.12) | copy-start | bytes 1540
  60.0 52.3 %copy-start.2 = (s32[768]{0:T(1024)S(1)}, s32[768]{0:T(1024)}, u32[]{:S(2)}) copy-start(s32[768]{0:T(1024)} %param.11) | copy-start | bytes 9220
  102.8 48.4 %copy-start.3 = (s32[768]{0:T(1024)S(1)}, s32[768]{0:T(1024)}, u32[]{:S(2)}) copy-start(s32[768]{0:T(1024)} %param.13) | copy-start | bytes 9220
  109.7 157.7 %collective-permute-start.8 = (f32[1536,768]{1,0:T(8,128)}, f32[1536,768]{1,0:T(8,128)}, u32[]{:S(2)}, u32[]{:S(2)}) collective-permute-start(f32[1536,768]{1,0:T(8,128)} %bitcast.93), channel_id=1, source_target_pairs={{0,24},{8,0},{16,8},{24,16},{1,25},{9,1},{17,9},{25,17},{2,26},{10... | collective-permute-start | bytes 14155784 | tf_op jit(solution)/shard_map/ppermute | solution.py:36
  118.3 38.5 %all-to-all-start = ((s32[8,1,192]{2,1,0:T(1,128)}), s32[8,1,192]{2,1,0:T(1,128)S(1)}, u32[]{:S(2)}, u32[]{:S(2)}) async-start(s32[8,1,192]{2,1,0:T(1,128)} %all_to_all.14), calls=%async_computation | async-start | bytes 16384 | tf_op jit(solution)/shard_map/all_to_all | solution.py:103
  156.9 51.5 %collective-permute-start.7 = (s32[1536]{0:T(1024)S(1)}, s32[1536]{0:T(1024)S(1)}, u32[]{:S(2)}, u32[]{:S(2)}) collective-permute-start(s32[1536]{0:T(1024)S(1)} %reshape.136), channel_id=1, source_target_pairs={{0,24},{8,0},{16,8},{24,16},{1,25},{9,1},{17,9},{25,17},{2,26},{10... | collective-permute-start | bytes 18440 | tf_op jit(solution)/shard_map/ppermute | solution.py:36
  157.5 51.0 %collective-permute-start.10 = (s32[1536]{0:T(1024)S(1)}, s32[1536]{0:T(1024)S(1)}, u32[]{:S(2)}, u32[]{:S(2)}) collective-permute-start(s32[1536]{0:T(1024)S(1)} %reshape.136), channel_id=1, source_target_pairs={{0,16},{8,24},{16,0},{24,8},{1,17},{9,25},{17,1},{25,9},{2,18},{10... | collective-permute-start | bytes 18440 | tf_op jit(solution)/shard_map/ppermute | solution.py:36
  158.1 75.9 %copy-start.1 = (s32[8,1,192]{2,0,1:T(8,128)}, s32[8,1,192]{2,0,1:T(8,128)S(1)}, u32[]{:S(2)}) copy-start(s32[8,1,192]{2,0,1:T(8,128)S(1)} %copy.16) | copy-start | bytes 18436
  233.4 100.2 %collective-permute-start.11 = (f32[1536,768]{1,0:T(8,128)}, f32[1536,768]{1,0:T(8,128)}, u32[]{:S(2)}, u32[]{:S(2)}) collective-permute-start(f32[1536,768]{1,0:T(8,128)} %bitcast.94), channel_id=1, source_target_pairs={{0,16},{8,24},{16,0},{24,8},{1,17},{9,25},{17,1},{25,9},{2,18},{10... | collective-permute-start | bytes 14155784 | tf_op jit(solution)/shard_map/ppermute | solution.py:36
  300.2 66.3 %collective-permute-start.9 = (f32[1536]{0:T(1024)S(1)}, f32[1536]{0:T(1024)S(1)}, u32[]{:S(2)}, u32[]{:S(2)}) collective-permute-start(f32[1536]{0:T(1024)S(1)} %reshape.139), channel_id=1, source_target_pairs={{0,8},{8,16},{16,24},{24,0},{1,9},{9,17},{17,25},{25,1},{2,10},{10... | collective-permute-start | bytes 18440 | tf_op jit(solution)/shard_map/ppermute | solution.py:36
  367.2 35.0 %all-to-all-start.1 = ((f32[8,1,192]{2,1,0:T(1,128)}), f32[8,1,192]{2,1,0:T(1,128)S(1)}, u32[]{:S(2)}, u32[]{:S(2)}) async-start(f32[8,1,192]{2,1,0:T(1,128)} %all_to_all.17), calls=%async_computation.1 | async-start | bytes 16384 | tf_op jit(solution)/shard_map/all_to_all | solution.py:118
Sparse Core Ops, SparseCore 0:
  114.4 58.5 reduce-scatter.1
